TPU v7x, 32 devices: a whole 2x2x4 slice. The times are simulated.
32 devices in a mesh: scenes: 2 (over x), rows: 16 (over z, y, core).
Axes of the slice: x: 2, y: 2, z: 4, core: 2. Of those that a mesh axis runs over, the one named last changes fastest.
Arguments:
- images: float32 [64, 128, 128], P(('scenes', 'rows')), parts along dimension 0, may hold values from -6 to 6
- conv_weight: float32 [3, 3, 128, 128], replicated, may hold values from -0.1875 to 0.1875
- lift_weight: float32 [320, 128], replicated, may hold values from -0.5 to 0.5
- vol_weight: float32 [3, 3, 3, 32, 40], replicated, may hold values from -0.1875 to 0.1875
Outputs:
- filtered: float32 [64, 32, 48, 128], P(('scenes', 'rows')), parts along dimension 0
There are 2 independent parts, one for each index of `scenes`. A program takes and returns all parts, laid end to end along the dimension named above; an argument that names none is the same for every part. Nothing has to cross between parts.
All inputs are finite; a program needn't handle non-finite values.
Results may differ from a plain program's by a relative error of at most 0.0001.
Values sent between devices are 32-bit elements; how exact they have to be, the bound alone decides.
A program may use at most 128 MiB of HBM per device.

v0:
```python
import jax
import jax.numpy as jnp
from jax import lax
from jax.sharding import PartitionSpec as P

GROUPS = 40
DISP = 48


precise = lax.Precision.HIGHEST


def with_halo(x, sides, width):
    for axis, dim in sides:
        size, length = (lax.axis_size(axis), x.shape[dim])
        up = [(i, (i + 1) % size) for i in range(size)]
        down = [(j, i) for i, j in up]
        last = lax.slice_in_dim(x, length - width, length, axis=dim)
        first = lax.slice_in_dim(x, 0, width, axis=dim)
        before = lax.ppermute(last, axis, up)
        after = lax.ppermute(first, axis, down)
        x = jnp.concatenate([before, x, after], axis=dim)
    return x


def passed_along(x, axis, by):
    size = lax.axis_size(axis)
    return lax.ppermute(x, axis, [(i, (i + by) % size) for i in range(size)])


def conv_plane(planes, weight, padding):
    result = lax.conv_general_dilated(
        planes[None],
        weight,
        (1, 1),
        padding,
        dimension_numbers=("NHCW", "HWOI", "NHCW"),
        precision=precise,
    )
    return result[0]


def lift_features(weight, hidden):
    return jnp.einsum("fi,ric->rfc", weight, hidden, precision=precise)


def correlate(anchor, other, groups, disparities):
    row_count, channels, columns = anchor.shape
    padded = jnp.pad(other, ((0, 0), (0, 0), (disparities, 0)))
    layers = []
    for offset in range(disparities):
        shifted = padded[:, :, disparities - offset : disparities - offset + columns]
        product = (anchor * shifted).reshape(row_count, groups, channels // groups, columns)
        layers.append(jnp.mean(product, axis=2))
    return jnp.stack(layers, axis=2)


def conv_volume(volume, weight, padding):
    result = lax.conv_general_dilated(
        volume[None],
        weight,
        (1, 1, 1),
        padding,
        dimension_numbers=("NHCDW", "HDWOI", "NHCDW"),
        precision=precise,
    )
    return result[0]


def clip_rim(padded, axis_dim, position, quarter):
    extent = padded.shape[axis_dim]
    place = jnp.arange(extent)
    starts = (position == quarter) | (position == 3 * quarter)
    ends = (position == quarter - 1) | (position == 3 * quarter - 1)
    dropped = (place == 0) & starts | (place == extent - 1) & ends
    mask_shape = [1] * padded.ndim
    mask_shape[axis_dim] = extent
    return padded * jnp.where(dropped, 0.0, 1.0).astype(padded.dtype).reshape(mask_shape)


def on_device(images, conv_weight, lift_weight, vol_weight):
    devices = lax.axis_size("rows")
    position = lax.axis_index("rows")
    halfway = devices // 2
    quarter = devices // 4
    framed = with_halo(images, (("rows", 0),), 1)
    framed = clip_rim(framed, 0, position, quarter)
    hidden = jax.nn.relu(conv_plane(framed, conv_weight, ((0, 0), (1, 1))))
    features = lift_features(lift_weight, hidden)
    partner = lift_features(lift_weight, passed_along(hidden, "rows", halfway))
    is_right = (position < quarter) | (position >= 3 * quarter)

    def orient(values):
        return jnp.where(is_right, jnp.flip(values, -1), values)

    volume = orient(correlate(orient(features), orient(partner), GROUPS, DISP))
    volume = with_halo(volume, (("rows", 0),), 1)
    volume = clip_rim(volume, 0, position, quarter)
    return conv_volume(volume, vol_weight, ((0, 0), (1, 1), (1, 1)))


def solution(mesh):
    placed = (P(("scenes", "rows"), None, None), P(), P(), P())
    return jax.shard_map(
        on_device,
        mesh=mesh,
        in_specs=placed,
        out_specs=P(("scenes", "rows"), None, None, None),
        check_vma=False,
    )
```

profile of v0, /device:TPU:1, one launch (start us, length us, event | category | flops | bytes accessed | tf_op | source)
XLA Modules:
  0.0 253.1 jit_solution(3526295873962544792)
XLA Ops:
  0.0 0.9 fusion.168
  1.0 2.7 %collective-permute-start = (f32[1,128,128]{2,1,0:T(8,128)S(1)}, f32[1,128,128]{2,1,0:T(8,128)S(1)}, u32[]{:S(2)}, u32[]{:S(2)}) collective-permute-start(f32[1,128,128]{2,1,0:T(8,128)S(1)} %get-tuple-element.56), channel_id=1, source_target_pairs={{0,1},{1,2},{2,3},{3,4},{4,5},{5,6},{6,7},{7,8},{8,9},{9,10},{10,1... | collective-permute-start | bytes 196616 | tf_op jit(solution)/shard_map/ppermute | solution.py:20
  3.6 1.3 collective-permute-done
  5.0 3.1 %collective-permute-done.1 = f32[1,128,128]{2,1,0:T(8,128)S(1)} collective-permute-done((f32[1,128,128]{2,1,0:T(8,128)S(1)}, f32[1,128,128]{2,1,0:T(8,128)S(1)}, u32[]{:S(2)}, u32[]{:S(2)}) %collective-permute-start.1) | collective-permute-done | bytes 65568 | tf_op jit(solution)/shard_map/ppermute | solution.py:21
  8.1 1.0 fusion.156
  9.4 1.2 fusion.10
  10.7 1.6 collective-permute-start.2
  13.7 6.0 %collective-permute-done.2 = f32[2,128,128]{2,1,0:T(8,128)S(1)} collective-permute-done((f32[2,128,128]{2,1,0:T(8,128)S(1)}, f32[2,128,128]{2,1,0:T(8,128)S(1)}, u32[]{:S(2)}, u32[]{:S(2)}) %collective-permute-start.2) | collective-permute-done | bytes 131104 | tf_op jit(solution)/shard_map/ppermute | solution.py:28
  21.0 1.9 fusion.151
  22.9 1.2 fusion.43
  24.1 1.8 fusion.97
  26.6 2.5 %rev.13 = f32[2,40,48,128]{3,1,0,2:T(8,128)} reverse(f32[2,40,48,128]{3,1,0,2:T(8,128)S(1)} %constant_dynamic-update-slice_fusion), dimensions={3} | reverse | bytes 3932160 | tf_op jit(solution)/shard_map/jit(_flip)/rev | solution.py:94
  29.1 1.8 broadcast_select_fusion.1
  32.0 20.8 %collective-permute-done.3 = f32[1,40,48,128]{3,1,2,0:T(8,128)S(1)} collective-permute-done((f32[1,40,48,128]{3,1,2,0:T(8,128)S(1)}, f32[1,40,48,128]{3,1,2,0:T(8,128)S(1)}, u32[]{:S(2)}, u32[]{:S(2)}) %collective-permute-start.3) | collective-permute-done | bytes 983072 | tf_op jit(solution)/shard_map/ppermute | solution.py:20
  52.7 2.5 %collective-permute-done.4 = f32[1,40,48,128]{3,1,0,2:T(8,128)S(1)} collective-permute-done((f32[1,40,48,128]{3,1,0,2:T(8,128)S(1)}, f32[1,40,48,128]{3,1,0,2:T(8,128)S(1)}, u32[]{:S(2)}, u32[]{:S(2)}) %collective-permute-start.4) | collective-permute-done | bytes 983072 | tf_op jit(solution)/shard_map/ppermute | solution.py:21
  55.2 2.6 %fusion.7 = f32[4,40,48,1,128]{4,1,0,2,3:T(8,128)} fusion(f32[1,1,40,48,128]{4,2,1,3,0:T(8,128)S(1)} %bitcast.341, f32[1,2,40,48,128]{4,2,1,3,0:T(8,128)S(1)} %bitcast.337, f32[1,1,40,48,128]{4,2,1,3,0:T(8,128)S(1)} %bitcast.340, f32[4]{0:T(128)S(1)} %or_select_fusion), kind=kLoop, calls=%fused_computation.57 | loop fusion | flops 2949120 | bytes 7864336 | tf_op jit(solution)/shard_map/mul | solution.py:78
  57.8 8.2 %copy.123 = f32[4,40,48,1,128]{2,1,4,0,3:T(8,128)} copy(f32[4,40,48,1,128]{4,1,0,2,3:T(8,128)} %fusion.7) | data formatting | bytes 7864320
  66.1 8.8 %pad.7.clone = f32[4,40,48,1,136]{2,1,4,0,3:T(8,128)} pad(f32[4,40,48,1,128]{2,1,4,0,3:T(8,128)} %copy.123, f32[]{:T(128)} %constant.70.clone.1), padding=0_0x0_0x0_0x0_0x1_7 | pad | bytes 8110084 | tf_op jit(solution)/shard_map/mul | solution.py:78
  74.9 14.0 %copy.117 = f32[4,40,48,1,8,17]{1,4,5,2,0,3:T(8,128)} copy(f32[4,40,48,1,8,17]{2,1,5,4,0,3:T(8,128)} %bitcast.336) | data formatting | bytes 8355840 | tf_op jit(solution)/shard_map/conv_general_dilated | solution.py:59
  88.8 1.6 slice.213
  90.5 147.0 %broadcast_select_fusion = f32[2,48,8,17,32]{4,2,3,1,0:T(8,128)} fusion(pred[8,17]{0,1:T(8,128)(4,1)S(1)} %copy-done.3, f32[3,3,3,32,40]{4,3,2,1,0:T(8,128)S(1)} %copy-done.4, f32[4,40,48,1,7,2]{1,4,5,2,0,3:T(8,128)S(1)} %slice.213, f32[4,40,48,1,8,17]{1,4,5,2,0,3:T(8,128)} %copy.117), kind=kOutput, calls=%fused_computation.58 | convolution fusion | flops 5343301632 | bytes 6417544 | tf_op jit(solution)/shard_map/conv_general_dilated | solution.py:59
  237.5 6.4 %copy.118 = f32[2,48,8,17,32]{1,4,3,2,0:T(8,128)} copy(f32[2,48,8,17,32]{4,2,3,1,0:T(8,128)} %broadcast_select_fusion) | data formatting | bytes 3342336 | tf_op jit(solution)/shard_map/conv_general_dilated | solution.py:59
  243.8 4.7 %slice_bitcast_fusion = f32[2,32,48,128]{2,1,3,0:T(8,128)} fusion(f32[2,48,1,136,32]{1,4,3,0,2:T(8,128)} %bitcast.338), kind=kLoop, calls=%fused_computation.55 | loop fusion | bytes 3145728 | tf_op jit(solution)/shard_map/squeeze | solution.py:67
  248.5 4.6 %copy.119 = f32[2,32,48,128]{3,2,1,0:T(8,128)} copy(f32[2,32,48,128]{2,1,3,0:T(8,128)} %slice_bitcast_fusion) | data formatting | bytes 3145728 | tf_op jit(solution)/shard_map/squeeze | solution.py:67
  (75 shorter events, 4.3 us)
Async XLA Ops:
  0.0 9.3 %copy-start = (f32[3,3,128,128]{3,2,1,0:T(8,128)S(1)}, f32[3,3,128,128]{3,2,1,0:T(8,128)}, u32[]{:S(2)}) copy-start(f32[3,3,128,128]{3,2,1,0:T(8,128)} %param.5) | copy-start | bytes 1769476
  0.0 9.3 %copy-start.3 = (pred[8,17]{0,1:T(8,128)(4,1)S(1)}, pred[8,17]{0,1:T(8,128)(4,1)}, u32[]{:S(2)}) copy-start(pred[8,17]{0,1:T(8,128)(4,1)} %constant.84) | copy-start | bytes 412
  1.0 4.0 %collective-permute-start = (f32[1,128,128]{2,1,0:T(8,128)S(1)}, f32[1,128,128]{2,1,0:T(8,128)S(1)}, u32[]{:S(2)}, u32[]{:S(2)}) collective-permute-start(f32[1,128,128]{2,1,0:T(8,128)S(1)} %get-tuple-element.56), channel_id=1, source_target_pairs={{0,1},{1,2},{2,3},{3,4},{4,5},{5,6},{6,7},{7,8},{8,9},{9,10},{10,1... | collective-permute-start | bytes 196616 | tf_op jit(solution)/shard_map/ppermute | solution.py:20
  3.6 4.4 %collective-permute-start.1 = (f32[1,128,128]{2,1,0:T(8,128)S(1)}, f32[1,128,128]{2,1,0:T(8,128)S(1)}, u32[]{:S(2)}, u32[]{:S(2)}) collective-permute-start(f32[1,128,128]{2,1,0:T(8,128)S(1)} %get-tuple-element.57), channel_id=1, source_target_pairs={{1,0},{2,1},{3,2},{4,3},{5,4},{6,5},{7,6},{8,7},{9,8},{10,9},{11,1... | collective-permute-start | bytes 196616 | tf_op jit(solution)/shard_map/ppermute | solution.py:21
  8.1 4.3 %copy-start.2 = (f32[320,128]{1,0:T(8,128)S(1)}, f32[320,128]{1,0:T(8,128)}, u32[]{:S(2)}) copy-start(f32[320,128]{1,0:T(8,128)} %param.6) | copy-start | bytes 491524
  10.7 8.9 %collective-permute-start.2 = (f32[2,128,128]{2,1,0:T(8,128)S(1)}, f32[2,128,128]{2,1,0:T(8,128)S(1)}, u32[]{:S(2)}, u32[]{:S(2)}) collective-permute-start(f32[2,128,128]{2,1,0:T(8,128)S(1)} %bitcast.344), channel_id=1, source_target_pairs={{0,8},{1,9},{2,10},{3,11},{4,12},{5,13},{6,14},{7,15},{8,0},{9,1},... | collective-permute-start | bytes 393224 | tf_op jit(solution)/shard_map/ppermute | solution.py:28
  31.1 21.6 %collective-permute-start.3 = (f32[1,40,48,128]{3,1,2,0:T(8,128)S(1)}, f32[1,40,48,128]{3,1,2,0:T(8,128)S(1)}, u32[]{:S(2)}, u32[]{:S(2)}) collective-permute-start(f32[1,40,48,128]{3,1,2,0:T(8,128)S(1)} %get-tuple-element.54), channel_id=1, source_target_pairs={{0,1},{1,2},{2,3},{3,4},{4,5},{5,6},{6,7},{7,8},{8,9},{9,10},{10,1... | collective-permute-start | bytes 2949128 | tf_op jit(solution)/shard_map/ppermute | solution.py:20
  31.1 24.1 %collective-permute-start.4 = (f32[1,40,48,128]{3,1,0,2:T(8,128)S(1)}, f32[1,40,48,128]{3,1,0,2:T(8,128)S(1)}, u32[]{:S(2)}, u32[]{:S(2)}) collective-permute-start(f32[1,40,48,128]{3,1,0,2:T(8,128)S(1)} %get-tuple-element.55), channel_id=1, source_target_pairs={{1,0},{2,1},{3,2},{4,3},{5,4},{6,5},{7,6},{8,7},{9,8},{10,9},{11,1... | collective-permute-start | bytes 2949128 | tf_op jit(solution)/shard_map/ppermute | solution.py:21
  88.8 1.7 copy-start.4
  243.8 9.3 %copy-start.1 = (f32[3,3,128,128]{3,2,1,0:T(8,128)S(1)}, f32[3,3,128,128]{3,2,1,0:T(8,128)}, u32[]{:S(2)}) copy-start(f32[3,3,128,128]{3,2,1,0:T(8,128)} %param.5) | copy-start | bytes 1769476
where the time goes:
time: 254 us; the launch traced here: 253 us
  matrix products  149 us (59%)
  local copies, waits for them, and re-layouts  54 us (21%)
  waiting for transfers between devices  33.7 us (13%)
  other arithmetic  10.7 us (4%)
  starting transfers between devices  5.18 us (2%)
    conv_general_dilated x1, matrix products, conv_volume(): lax.conv_general_dilated(volume[None], weight, (1, 1, 1), padding, dimens...  147 us
    ppermute x2, waiting for transfers between devices, with_halo(): before = lax.ppermute(last, axis, up)  22.1 us
    conv_general_dilated x3, local copies, waits for them, and re-layouts, conv_volume(): lax.conv_general_dilated(volume[None], weight, (1, 1, 1), padding, dimens...  22 us
    squeeze x2, local copies, waits for them, and re-layouts, conv_volume(): return result[0]  9.29 us
    mul x2, local copies, waits for them, and re-layouts, clip_rim(): padded * jnp.where(dropped, 0.0, 1.0).astype(padded.dtype).reshape(mask_s...  8.84 us
    unnamed x14, local copies, waits for them, and re-layouts  8.62 us
    ppermute x1, waiting for transfers between devices, passed_along(): return lax.ppermute(x, axis, [(i, (i + by) % size) for i in range(size)])  5.98 us
    ppermute x2, waiting for transfers between devices, with_halo(): after = lax.ppermute(first, axis, down)  5.64 us
  transfers between devices with their start and end apart: 5, of which 5 were waited for; matrix products, arithmetic and copies ran while one was open for 1% of the time, Pallas kernels for 0%

commit v1 on v0

v1 whole, which is shorter than its diff:
```python
import functools

import jax
import jax.numpy as jnp
from jax import lax
from jax.experimental import pallas as pl
from jax.experimental.pallas import tpu as pltpu
from jax.sharding import PartitionSpec as P

DISP = 48
LANES = 128
f32, bf16 = jnp.float32, jnp.bfloat16


def split(x):
    hi = x.astype(bf16)
    return hi, (x - hi.astype(f32)).astype(bf16)


def dot(a, b):
    return jnp.dot(a, b, preferred_element_type=f32)


def dot3(stacked, rows, hi, lo):
    both = dot(stacked, hi)
    return both[:rows] + both[rows:] + dot(stacked[:rows], lo)


def taps(y, size, lane):
    cols = y.shape[1]
    before = jnp.where(lane >= 1, pltpu.roll(y[:size], 1, 1), 0.0)
    after = jnp.where(lane < cols - 1, pltpu.roll(y[2 * size :], cols - 1, 1), 0.0)
    return y[size : 2 * size] + before + after


def compute(own, other, cw, lw, vw, out, feat_a, feat_b, cost_hi, cost_lo, vol_f, vol_2):
    position = lax.axis_index("rows")
    devices = lax.axis_size("rows")
    quarter = devices // 4
    starts = (position == quarter) | (position == 3 * quarter)
    ends = (position == quarter - 1) | (position == 3 * quarter - 1)
    is_right = (position < quarter) | (position >= 3 * quarter)

    framed, cin, cols = own.shape
    rows = framed - 4
    halo = rows + 2
    feat = lw.shape[0]
    outc, groups = vw.shape[3:]
    per = feat // groups
    depth = halo * groups
    used = 3 * depth
    padded = vol_f.shape[1]
    lane = lax.broadcasted_iota(jnp.int32, (1, cols), 1)

    vol_f[...] = jnp.zeros_like(vol_f)
    for dd in range(3):
        for dc in range(3):
            for r in range(rows):
                for dr in range(3):
                    top = (dc * rows + r) * outc
                    left = dd * depth + (r + dr) * groups
                    vol_f[top : top + outc, left : left + groups] = vw[dr, dd, dc] * (1.0 / per)
    high, low = split(vol_f[...])
    m = 3 * rows * outc
    vol_2[:m] = high
    vol_2[m:] = low

    wide = jnp.concatenate([cw[dr].reshape(3 * cin, cin) for dr in range(3)], axis=1)
    conv_2 = jnp.concatenate(split(wide), axis=0)
    lift = jnp.concatenate([lw[pl.ds(k, groups, stride=per), :] for k in range(per)], axis=0)
    lift_2 = jnp.concatenate(split(lift), axis=0)
    parts = []
    for s in range(framed):
        x = jnp.concatenate([own[s], other[s]], axis=1)
        if s < 2:
            x = jnp.where(starts, 0.0, x)
        if s >= rows + 2:
            x = jnp.where(ends, 0.0, x)
        parts.append(split(x))
    for r in range(halo):
        hi = jnp.concatenate([parts[r + k][0] for k in range(3)], axis=0)
        lo = jnp.concatenate([parts[r + k][1] for k in range(3)], axis=0)
        y = dot3(conv_2, 3 * cin, hi, lo)
        here = jnp.maximum(taps(y[:, :cols], cin, lane), 0.0)
        there = jnp.maximum(taps(y[:, cols:], cin, lane), 0.0)
        if r == 0:
            here = jnp.where(starts, 0.0, here)
        if r == halo - 1:
            here = jnp.where(ends, 0.0, here)
        f = dot3(lift_2, feat, *split(jnp.concatenate([here, there], axis=1)))
        for k in range(per):
            feat_a[k, r * groups : (r + 1) * groups, :] = f[k * groups : (k + 1) * groups, :cols]
            feat_b[k, r * groups : (r + 1) * groups, :] = f[k * groups : (k + 1) * groups, cols:]

    for buf in (cost_hi, cost_lo):
        buf[:depth] = jnp.zeros((depth, cols), bf16)
        tail = buf.shape[0] - (DISP + 1) * depth
        buf[(DISP + 1) * depth :] = jnp.zeros((tail, cols), bf16)
    reach = jnp.where(is_right, cols - 1 - lane, lane)

    @pl.loop(0, depth // 16)
    def _(j):
        base = pl.multiple_of(j * 16, 16)
        a = [feat_a[k, pl.ds(base, 16), :] for k in range(per)]
        b = [feat_b[k, pl.ds(base, 16), :] for k in range(per)]

        def at(d, carry):
            shift = jnp.where(is_right, lax.rem(cols - d, cols), d)
            total = a[0] * pltpu.roll(b[0], shift, 1)
            for k in range(1, per):
                total += a[k] * pltpu.roll(b[k], shift, 1)
            hi, lo = split(jnp.where(reach >= d, total, 0.0))
            place = pl.ds(pl.multiple_of((d + 1) * depth + base, 16), 16)
            cost_hi[place, :] = hi
            cost_lo[place, :] = lo
            return carry

        lax.fori_loop(0, DISP, at, 0, unroll=4)

    @pl.loop(0, DISP // 2)
    def _(pair):
        d = pair * 2
        first = pl.ds(pl.multiple_of(d * depth, 16), padded)
        second = pl.ds(pl.multiple_of((d + 1) * depth, 16), padded)
        hi = jnp.concatenate([cost_hi[first, :], cost_hi[second, :]], axis=1)
        lo = jnp.concatenate([cost_lo[first, :], cost_lo[second, :]], axis=1)
        y = dot3(vol_2[...], m, hi, lo)
        for h in range(2):
            z = taps(y[:, h * cols : (h + 1) * cols], rows * outc, lane)
            out[pl.ds(d + h, rows * outc, stride=DISP), :] = z


def shifted(x, by):
    size = lax.axis_size("rows")
    return lax.ppermute(x, "rows", [(i, (i + by) % size) for i in range(size)])


def framed(x):
    return jnp.concatenate([shifted(x[-2:], 1), x, shifted(x[:2], -1)], axis=0)


def on_device(images, conv_weight, lift_weight, vol_weight):
    rows, _, cols = images.shape
    outc, groups = vol_weight.shape[3:]
    per = lift_weight.shape[0] // groups
    depth = (rows + 2) * groups
    padded = -(-3 * depth // 256) * 256
    m = 3 * rows * outc
    length = (DISP + 1) * depth - 2 * depth + padded + depth
    own = framed(images)
    other = framed(shifted(images, lax.axis_size("rows") // 2))
    vmem = pl.BlockSpec(memory_space=pltpu.VMEM)
    flat = pl.pallas_call(
        compute,
        out_shape=jax.ShapeDtypeStruct((rows * outc * DISP, cols), f32),
        in_specs=[vmem] * 5,
        out_specs=vmem,
        scratch_shapes=[
            pltpu.VMEM((per, depth, cols), f32),
            pltpu.VMEM((per, depth, cols), f32),
            pltpu.VMEM((length, cols), bf16),
            pltpu.VMEM((length, cols), bf16),
            pltpu.VMEM((m, padded), f32),
            pltpu.VMEM((2 * m, padded), bf16),
        ],
        compiler_params=pltpu.CompilerParams(vmem_limit_bytes=48 << 20),
    )(own, other, conv_weight, lift_weight, vol_weight)
    return flat.reshape(rows, outc, DISP, cols)


def solution(mesh):
    placed = (P(("scenes", "rows"), None, None), P(), P(), P())
    return jax.shard_map(
        on_device,
        mesh=mesh,
        in_specs=placed,
        out_specs=P(("scenes", "rows"), None, None, None),
        check_vma=False,
    )
```

time: 254 us -> 54.2 us (0.21)
  the two profiles are of different devices: /device:TPU:1 before, /device:TPU:0 now
where the time goes in v1:
time: 54.2 us; the launch traced here: 54.1 us
  Pallas kernels  32.2 us (59%)
  waiting for transfers between devices  11.3 us (21%)
  starting transfers between devices  9.63 us (18%)
  other arithmetic  0.96 us (2%)
    pallas_call x1, Pallas kernels, on_device(): pl.pallas_call(compute, out_shape=jax.ShapeDtypeStruct((rows * outc * DIS...  32.2 us
    ppermute x5, waiting for transfers between devices, shifted(): return lax.ppermute(x, 'rows', [(i, (i + by) % size) for i in range(size)])  11.3 us
    ppermute x5, starting transfers between devices, shifted(): return lax.ppermute(x, 'rows', [(i, (i + by) % size) for i in range(size)])  9.63 us
  transfers between devices with their start and end apart: 5, of which 3 were waited for; matrix products, arithmetic and copies ran while one was open for 2% of the time, Pallas kernels for 0%

profile of v1, /device:TPU:0, one launch (start us, length us, event | category | flops | bytes accessed | tf_op | source)
XLA Modules:
  0.0 54.1 jit_solution(16844526124524420564)
XLA Ops:
  0.0 0.0 copy-start.1
  0.0 0.0 copy-start.2
  0.0 0.0 copy-start
  0.0 4.1 %collective-permute-start.2 = (f32[2,128,128]{2,1,0:T(8,128)}, f32[2,128,128]{2,1,0:T(8,128)S(1)}, u32[]{:S(2)}, u32[]{:S(2)}) collective-permute-start(f32[2,128,128]{2,1,0:T(8,128)} %param.4), channel_id=1, source_target_pairs={{0,8},{1,9},{2,10},{3,11},{4,12},{5,13},{6,14},{7,15},{8,0},{9,1},... | collective-permute-start | bytes 393224 | tf_op jit(solution)/shard_map/ppermute | solution.py:135
  4.1 1.5 %collective-permute-start.1 = (f32[2,128,128]{2,1,0:T(8,128)}, f32[2,128,128]{2,1,0:T(8,128)S(1)}, u32[]{:S(2)}, u32[]{:S(2)}) collective-permute-start(f32[2,128,128]{2,1,0:T(8,128)} %param.4), channel_id=1, source_target_pairs={{0,15},{1,0},{2,1},{3,2},{4,3},{5,4},{6,5},{7,6},{8,7},{9,8},{10,9... | collective-permute-start | bytes 393224 | tf_op jit(solution)/shard_map/ppermute | solution.py:135
  5.6 0.0 collective-permute-start
  5.6 5.1 %collective-permute-done.2 = f32[2,128,128]{2,1,0:T(8,128)S(1)} collective-permute-done((f32[2,128,128]{2,1,0:T(8,128)}, f32[2,128,128]{2,1,0:T(8,128)S(1)}, u32[]{:S(2)}, u32[]{:S(2)}) %collective-permute-start.2) | collective-permute-done | bytes 131104 | tf_op jit(solution)/shard_map/ppermute | solution.py:135
  10.8 4.0 %collective-permute-start.4 = (f32[2,128,128]{2,1,0:T(8,128)S(1)}, f32[2,128,128]{2,1,0:T(8,128)S(1)}, u32[]{:S(2)}, u32[]{:S(2)}) collective-permute-start(f32[2,128,128]{2,1,0:T(8,128)S(1)} %collective-permute-done.2), channel_id=1, source_target_pairs={{0,15},{1,0},{2,1},{3,2},{4,3},{5,4},{6,5},{7,6},{8,7},{9,8},{10,9... | collective-permute-start | bytes 393224 | tf_op jit(solution)/shard_map/ppermute | solution.py:135
  14.8 0.0 collective-permute-start.3
  14.8 0.0 collective-permute-done.1
  14.8 0.0 collective-permute-done
  14.8 0.9 %pad_maximum_fusion.own = f32[6,128,128]{2,1,0:T(8,128)S(1)} fusion(f32[2,128,128]{2,1,0:T(8,128)S(1)} %collective-permute-done.1, f32[2,128,128]{2,1,0:T(8,128)} %param.4, f32[2,128,128]{2,1,0:T(8,128)S(1)} %collective-permute-done), kind=kLoop, calls=%fused_computation | loop fusion | flops 196608 | bytes 786432 | tf_op jit(solution)/shard_map/concatenate | solution.py:139
  15.7 1.6 %collective-permute-done.4 = f32[2,128,128]{2,1,0:T(8,128)S(1)} collective-permute-done((f32[2,128,128]{2,1,0:T(8,128)S(1)}, f32[2,128,128]{2,1,0:T(8,128)S(1)}, u32[]{:S(2)}, u32[]{:S(2)}) %collective-permute-start.4) | collective-permute-done | bytes 131104 | tf_op jit(solution)/shard_map/ppermute | solution.py:135
  17.3 4.6 %collective-permute-done.3 = f32[2,128,128]{2,1,0:T(8,128)S(1)} collective-permute-done((f32[2,128,128]{2,1,0:T(8,128)S(1)}, f32[2,128,128]{2,1,0:T(8,128)S(1)}, u32[]{:S(2)}, u32[]{:S(2)}) %collective-permute-start.3) | collective-permute-done | bytes 131104 | tf_op jit(solution)/shard_map/ppermute | solution.py:135
  21.9 0.0 copy-done.1
  21.9 0.0 copy-done.2
  21.9 0.0 copy-done
  21.9 32.2 %shard_map.46 = f32[3072,128]{1,0:T(8,128)} custom-call(f32[6,128,128]{2,1,0:T(8,128)S(1)} %pad_maximum_fusion.own, f32[6,128,128]{2,1,0:T(8,128)S(1)} %pad_maximum_fusion.1.other, f32[3,3,128,128]{3,2,1,0:T(8,128)S(1)} %copy-done, f32[320,128]{1,0:T(8,128)S(1)} %copy-done.2, f32[3,3,3,32,40]{4,3,2,1,0:T(8,128)S(1)} %copy-done.1), custom_call_target="tpu_custom_call" | custom-call | tf_op jit(solution)/shard_map/pallas_call | solution.py:153
  (1 shorter events, 0.0 us)
Async XLA Ops:
  0.0 21.9 %copy-start.1 = (f32[3,3,3,32,40]{4,3,2,1,0:T(8,128)S(1)}, f32[3,3,3,32,40]{4,3,2,1,0:T(8,128)}, u32[]{:S(2)}) copy-start(f32[3,3,3,32,40]{4,3,2,1,0:T(8,128)} %vw.1) | copy-start | bytes 414724
  0.0 21.9 %copy-start.2 = (f32[320,128]{1,0:T(8,128)S(1)}, f32[320,128]{1,0:T(8,128)}, u32[]{:S(2)}) copy-start(f32[320,128]{1,0:T(8,128)} %lw.1) | copy-start | bytes 491524
  0.0 21.9 %copy-start = (f32[3,3,128,128]{3,2,1,0:T(8,128)S(1)}, f32[3,3,128,128]{3,2,1,0:T(8,128)}, u32[]{:S(2)}) copy-start(f32[3,3,128,128]{3,2,1,0:T(8,128)} %cw.1) | copy-start | bytes 1769476
  0.0 10.7 %collective-permute-start.2 = (f32[2,128,128]{2,1,0:T(8,128)}, f32[2,128,128]{2,1,0:T(8,128)S(1)}, u32[]{:S(2)}, u32[]{:S(2)}) collective-permute-start(f32[2,128,128]{2,1,0:T(8,128)} %param.4), channel_id=1, source_target_pairs={{0,8},{1,9},{2,10},{3,11},{4,12},{5,13},{6,14},{7,15},{8,0},{9,1},... | collective-permute-start | bytes 393224 | tf_op jit(solution)/shard_map/ppermute | solution.py:135
  4.1 10.6 %collective-permute-start.1 = (f32[2,128,128]{2,1,0:T(8,128)}, f32[2,128,128]{2,1,0:T(8,128)S(1)}, u32[]{:S(2)}, u32[]{:S(2)}) collective-permute-start(f32[2,128,128]{2,1,0:T(8,128)} %param.4), channel_id=1, source_target_pairs={{0,15},{1,0},{2,1},{3,2},{4,3},{5,4},{6,5},{7,6},{8,7},{9,8},{10,9... | collective-permute-start | bytes 393224 | tf_op jit(solution)/shard_map/ppermute | solution.py:135
  5.6 9.2 %collective-permute-start = (f32[2,128,128]{2,1,0:T(8,128)}, f32[2,128,128]{2,1,0:T(8,128)S(1)}, u32[]{:S(2)}, u32[]{:S(2)}) collective-permute-start(f32[2,128,128]{2,1,0:T(8,128)} %param.4), channel_id=1, source_target_pairs={{0,1},{1,2},{2,3},{3,4},{4,5},{5,6},{6,7},{7,8},{8,9},{9,10},{10,1... | collective-permute-start | bytes 393224 | tf_op jit(solution)/shard_map/ppermute | solution.py:135
  10.8 6.5 %collective-permute-start.4 = (f32[2,128,128]{2,1,0:T(8,128)S(1)}, f32[2,128,128]{2,1,0:T(8,128)S(1)}, u32[]{:S(2)}, u32[]{:S(2)}) collective-permute-start(f32[2,128,128]{2,1,0:T(8,128)S(1)} %collective-permute-done.2), channel_id=1, source_target_pairs={{0,15},{1,0},{2,1},{3,2},{4,3},{5,4},{6,5},{7,6},{8,7},{9,8},{10,9... | collective-permute-start | bytes 393224 | tf_op jit(solution)/shard_map/ppermute | solution.py:135
  14.8 7.1 %collective-permute-start.3 = (f32[2,128,128]{2,1,0:T(8,128)S(1)}, f32[2,128,128]{2,1,0:T(8,128)S(1)}, u32[]{:S(2)}, u32[]{:S(2)}) collective-permute-start(f32[2,128,128]{2,1,0:T(8,128)S(1)} %collective-permute-done.2), channel_id=1, source_target_pairs={{0,1},{1,2},{2,3},{3,4},{4,5},{5,6},{6,7},{7,8},{8,9},{9,10},{10,1... | collective-permute-start | bytes 393224 | tf_op jit(solution)/shard_map/ppermute | solution.py:135

commit v2 on v1

--- a/solution.py
+++ b/solution.py
@@ -8,6 +8,7 @@
 from jax.sharding import PartitionSpec as P
 
 DISP = 48
+CHUNK = 4
 LANES = 128
 f32, bf16 = jnp.float32, jnp.bfloat16
 
@@ -98,36 +99,36 @@
         buf[(DISP + 1) * depth :] = jnp.zeros((tail, cols), bf16)
     reach = jnp.where(is_right, cols - 1 - lane, lane)
 
-    @pl.loop(0, depth // 16)
-    def _(j):
-        base = pl.multiple_of(j * 16, 16)
-        a = [feat_a[k, pl.ds(base, 16), :] for k in range(per)]
-        b = [feat_b[k, pl.ds(base, 16), :] for k in range(per)]
+    def correlate(disparities):
+        shifts = [jnp.where(is_right, (cols - d) % cols, d) for d in disparities]
+        for base in range(0, depth, 16):
+            a = [feat_a[k, base : base + 16, :] for k in range(per)]
+            b = [feat_b[k, base : base + 16, :] for k in range(per)]
+            for d, shift in zip(disparities, shifts):
+                total = a[0] * pltpu.roll(b[0], shift, 1)
+                for k in range(1, per):
+                    total += a[k] * pltpu.roll(b[k], shift, 1)
+                hi, lo = split(jnp.where(reach >= d, total, 0.0))
+                place = (d + 1) * depth + base
+                cost_hi[place : place + 16, :] = hi
+                cost_lo[place : place + 16, :] = lo
 
-        def at(d, carry):
-            shift = jnp.where(is_right, lax.rem(cols - d, cols), d)
-            total = a[0] * pltpu.roll(b[0], shift, 1)
-            for k in range(1, per):
-                total += a[k] * pltpu.roll(b[k], shift, 1)
-            hi, lo = split(jnp.where(reach >= d, total, 0.0))
-            place = pl.ds(pl.multiple_of((d + 1) * depth + base, 16), 16)
-            cost_hi[place, :] = hi
-            cost_lo[place, :] = lo
-            return carry
-
-        lax.fori_loop(0, DISP, at, 0, unroll=4)
-
-    @pl.loop(0, DISP // 2)
-    def _(pair):
-        d = pair * 2
-        first = pl.ds(pl.multiple_of(d * depth, 16), padded)
-        second = pl.ds(pl.multiple_of((d + 1) * depth, 16), padded)
-        hi = jnp.concatenate([cost_hi[first, :], cost_hi[second, :]], axis=1)
-        lo = jnp.concatenate([cost_lo[first, :], cost_lo[second, :]], axis=1)
+    def filtered(d):
+        first, second = d * depth, (d + 1) * depth
+        hi, lo = [
+            jnp.concatenate([buf[first : first + padded, :], buf[second : second + padded, :]], axis=1)
+            for buf in (cost_hi, cost_lo)
+        ]
         y = dot3(vol_2[...], m, hi, lo)
         for h in range(2):
             z = taps(y[:, h * cols : (h + 1) * cols], rows * outc, lane)
             out[pl.ds(d + h, rows * outc, stride=DISP), :] = z
+
+    correlate(range(CHUNK + 2))
+    for d in range(0, DISP, CHUNK):
+        correlate(range(d + CHUNK + 2, min(d + 2 * CHUNK + 2, DISP)))
+        for e in range(d, d + CHUNK, 2):
+            filtered(e)
 
 
 def shifted(x, by):

time: 54.2 us -> 35.7 us (0.66)
  Pallas kernels: 32.2 us -> 13.6 us
    pallas_call x1, Pallas kernels: 32.2 us -> 13.6 us  [on_device(): pl.pallas_call(compute, out_shape=jax.ShapeDtypeStruct((rows * outc * DIS...]
  transfers between devices with their start and end apart: 5 -> 5, of which waited for: 3 -> 3; matrix products, arithmetic and copies ran while one was open for 2% -> 3% of each run, Pallas kernels for 0% -> 0%
where the time goes in v2:
time: 35.7 us; the launch traced here: 35.6 us
  Pallas kernels  13.6 us (38%)
  waiting for transfers between devices  11.3 us (32%)
  starting transfers between devices  9.63 us (27%)
  other arithmetic  0.96 us (3%)
    pallas_call x1, Pallas kernels, on_device(): pl.pallas_call(compute, out_shape=jax.ShapeDtypeStruct((rows * outc * DIS...  13.6 us
    ppermute x5, waiting for transfers between devices, shifted(): return lax.ppermute(x, 'rows', [(i, (i + by) % size) for i in range(size)])  11.3 us
    ppermute x5, starting transfers between devices, shifted(): return lax.ppermute(x, 'rows', [(i, (i + by) % size) for i in range(size)])  9.63 us
    concatenate x2, other arithmetic, framed(): return jnp.concatenate([shifted(x[-2:], 1), x, shifted(x[:2], -1)], axis=0)  0.96 us
  transfers between devices with their start and end apart: 5, of which 3 were waited for; matrix products, arithmetic and copies ran while one was open for 3% of the time, Pallas kernels for 0%

profile of v2, /device:TPU:0, one launch (start us, length us, event | category | flops | bytes accessed | tf_op | source)
XLA Modules:
  0.0 35.6 jit_solution(6519908549558855162)
XLA Ops:
  0.0 0.0 copy-start.1
  0.0 0.0 copy-start.2
  0.0 0.0 copy-start
  0.0 4.1 %collective-permute-start.2 = (f32[2,128,128]{2,1,0:T(8,128)}, f32[2,128,128]{2,1,0:T(8,128)S(1)}, u32[]{:S(2)}, u32[]{:S(2)}) collective-permute-start(f32[2,128,128]{2,1,0:T(8,128)} %param.4), channel_id=1, source_target_pairs={{0,8},{1,9},{2,10},{3,11},{4,12},{5,13},{6,14},{7,15},{8,0},{9,1},... | collective-permute-start | bytes 393224 | tf_op jit(solution)/shard_map/ppermute | solution.py:136
  4.1 1.5 %collective-permute-start.1 = (f32[2,128,128]{2,1,0:T(8,128)}, f32[2,128,128]{2,1,0:T(8,128)S(1)}, u32[]{:S(2)}, u32[]{:S(2)}) collective-permute-start(f32[2,128,128]{2,1,0:T(8,128)} %param.4), channel_id=1, source_target_pairs={{0,15},{1,0},{2,1},{3,2},{4,3},{5,4},{6,5},{7,6},{8,7},{9,8},{10,9... | collective-permute-start | bytes 393224 | tf_op jit(solution)/shard_map/ppermute | solution.py:136
  5.6 0.0 collective-permute-start
  5.6 5.1 %collective-permute-done.2 = f32[2,128,128]{2,1,0:T(8,128)S(1)} collective-permute-done((f32[2,128,128]{2,1,0:T(8,128)}, f32[2,128,128]{2,1,0:T(8,128)S(1)}, u32[]{:S(2)}, u32[]{:S(2)}) %collective-permute-start.2) | collective-permute-done | bytes 131104 | tf_op jit(solution)/shard_map/ppermute | solution.py:136
  10.8 4.0 %collective-permute-start.4 = (f32[2,128,128]{2,1,0:T(8,128)S(1)}, f32[2,128,128]{2,1,0:T(8,128)S(1)}, u32[]{:S(2)}, u32[]{:S(2)}) collective-permute-start(f32[2,128,128]{2,1,0:T(8,128)S(1)} %collective-permute-done.2), channel_id=1, source_target_pairs={{0,15},{1,0},{2,1},{3,2},{4,3},{5,4},{6,5},{7,6},{8,7},{9,8},{10,9... | collective-permute-start | bytes 393224 | tf_op jit(solution)/shard_map/ppermute | solution.py:136
  14.8 0.0 collective-permute-start.3
  14.8 0.0 collective-permute-done.1
  14.8 0.0 collective-permute-done
  14.8 0.9 %pad_maximum_fusion.own = f32[6,128,128]{2,1,0:T(8,128)S(1)} fusion(f32[2,128,128]{2,1,0:T(8,128)S(1)} %collective-permute-done.1, f32[2,128,128]{2,1,0:T(8,128)} %param.4, f32[2,128,128]{2,1,0:T(8,128)S(1)} %collective-permute-done), kind=kLoop, calls=%fused_computation | loop fusion | flops 196608 | bytes 786432 | tf_op jit(solution)/shard_map/concatenate | solution.py:140
  15.7 1.6 %collective-permute-done.4 = f32[2,128,128]{2,1,0:T(8,128)S(1)} collective-permute-done((f32[2,128,128]{2,1,0:T(8,128)S(1)}, f32[2,128,128]{2,1,0:T(8,128)S(1)}, u32[]{:S(2)}, u32[]{:S(2)}) %collective-permute-start.4) | collective-permute-done | bytes 131104 | tf_op jit(solution)/shard_map/ppermute | solution.py:136
  17.3 4.6 %collective-permute-done.3 = f32[2,128,128]{2,1,0:T(8,128)S(1)} collective-permute-done((f32[2,128,128]{2,1,0:T(8,128)S(1)}, f32[2,128,128]{2,1,0:T(8,128)S(1)}, u32[]{:S(2)}, u32[]{:S(2)}) %collective-permute-start.3) | collective-permute-done | bytes 131104 | tf_op jit(solution)/shard_map/ppermute | solution.py:136
  21.9 0.0 copy-done.1
  21.9 0.0 copy-done.2
  21.9 0.0 copy-done
  21.9 13.6 %shard_map.46 = f32[3072,128]{1,0:T(8,128)} custom-call(f32[6,128,128]{2,1,0:T(8,128)S(1)} %pad_maximum_fusion.own, f32[6,128,128]{2,1,0:T(8,128)S(1)} %pad_maximum_fusion.1.other, f32[3,3,128,128]{3,2,1,0:T(8,128)S(1)} %copy-done, f32[320,128]{1,0:T(8,128)S(1)} %copy-done.2, f32[3,3,3,32,40]{4,3,2,1,0:T(8,128)S(1)} %copy-done.1), custom_call_target="tpu_custom_call" | custom-call | tf_op jit(solution)/shard_map/pallas_call | solution.py:154
  (1 shorter events, 0.0 us)
Async XLA Ops:
  0.0 21.9 %copy-start.1 = (f32[3,3,3,32,40]{4,3,2,1,0:T(8,128)S(1)}, f32[3,3,3,32,40]{4,3,2,1,0:T(8,128)}, u32[]{:S(2)}) copy-start(f32[3,3,3,32,40]{4,3,2,1,0:T(8,128)} %vw.1) | copy-start | bytes 414724
  0.0 21.9 %copy-start.2 = (f32[320,128]{1,0:T(8,128)S(1)}, f32[320,128]{1,0:T(8,128)}, u32[]{:S(2)}) copy-start(f32[320,128]{1,0:T(8,128)} %lw.1) | copy-start | bytes 491524
  0.0 21.9 %copy-start = (f32[3,3,128,128]{3,2,1,0:T(8,128)S(1)}, f32[3,3,128,128]{3,2,1,0:T(8,128)}, u32[]{:S(2)}) copy-start(f32[3,3,128,128]{3,2,1,0:T(8,128)} %cw.1) | copy-start | bytes 1769476
  0.0 10.7 %collective-permute-start.2 = (f32[2,128,128]{2,1,0:T(8,128)}, f32[2,128,128]{2,1,0:T(8,128)S(1)}, u32[]{:S(2)}, u32[]{:S(2)}) collective-permute-start(f32[2,128,128]{2,1,0:T(8,128)} %param.4), channel_id=1, source_target_pairs={{0,8},{1,9},{2,10},{3,11},{4,12},{5,13},{6,14},{7,15},{8,0},{9,1},... | collective-permute-start | bytes 393224 | tf_op jit(solution)/shard_map/ppermute | solution.py:136
  4.1 10.6 %collective-permute-start.1 = (f32[2,128,128]{2,1,0:T(8,128)}, f32[2,128,128]{2,1,0:T(8,128)S(1)}, u32[]{:S(2)}, u32[]{:S(2)}) collective-permute-start(f32[2,128,128]{2,1,0:T(8,128)} %param.4), channel_id=1, source_target_pairs={{0,15},{1,0},{2,1},{3,2},{4,3},{5,4},{6,5},{7,6},{8,7},{9,8},{10,9... | collective-permute-start | bytes 393224 | tf_op jit(solution)/shard_map/ppermute | solution.py:136
  5.6 9.2 %collective-permute-start = (f32[2,128,128]{2,1,0:T(8,128)}, f32[2,128,128]{2,1,0:T(8,128)S(1)}, u32[]{:S(2)}, u32[]{:S(2)}) collective-permute-start(f32[2,128,128]{2,1,0:T(8,128)} %param.4), channel_id=1, source_target_pairs={{0,1},{1,2},{2,3},{3,4},{4,5},{5,6},{6,7},{7,8},{8,9},{9,10},{10,1... | collective-permute-start | bytes 393224 | tf_op jit(solution)/shard_map/ppermute | solution.py:136
  10.8 6.5 %collective-permute-start.4 = (f32[2,128,128]{2,1,0:T(8,128)S(1)}, f32[2,128,128]{2,1,0:T(8,128)S(1)}, u32[]{:S(2)}, u32[]{:S(2)}) collective-permute-start(f32[2,128,128]{2,1,0:T(8,128)S(1)} %collective-permute-done.2), channel_id=1, source_target_pairs={{0,15},{1,0},{2,1},{3,2},{4,3},{5,4},{6,5},{7,6},{8,7},{9,8},{10,9... | collective-permute-start | bytes 393224 | tf_op jit(solution)/shard_map/ppermute | solution.py:136
  14.8 7.1 %collective-permute-start.3 = (f32[2,128,128]{2,1,0:T(8,128)S(1)}, f32[2,128,128]{2,1,0:T(8,128)S(1)}, u32[]{:S(2)}, u32[]{:S(2)}) collective-permute-start(f32[2,128,128]{2,1,0:T(8,128)S(1)} %collective-permute-done.2), channel_id=1, source_target_pairs={{0,1},{1,2},{2,3},{3,4},{4,5},{5,6},{6,7},{7,8},{8,9},{9,10},{10,1... | collective-permute-start | bytes 393224 | tf_op jit(solution)/shard_map/ppermute | solution.py:136

commit v3 on v2

v3 whole, which is shorter than its diff:
```python
import jax
import jax.numpy as jnp
from jax import lax
from jax.experimental import pallas as pl
from jax.experimental.pallas import tpu as pltpu
from jax.sharding import PartitionSpec as P

DISP = 48
CHUNK = 4
STEP = 8
MESH = pl.DeviceIdType.MESH
f32, bf16 = jnp.float32, jnp.bfloat16


def split(x):
    hi = x.astype(bf16)
    return hi, (x - hi.astype(f32)).astype(bf16)


def dot(a, b):
    return jnp.dot(a, b, preferred_element_type=f32)


def dot3(stacked, rows, hi, lo):
    both = dot(stacked, hi)
    return both[:rows] + both[rows:] + dot(stacked[:rows], lo)


def taps(y, size, lane):
    cols = y.shape[1]
    before = jnp.where(lane >= 1, pltpu.roll(y[:size], 1, 1), 0.0)
    after = jnp.where(lane < cols - 1, pltpu.roll(y[2 * size :], cols - 1, 1), 0.0)
    return y[size : 2 * size] + before + after


def place_of():
    position = lax.axis_index("rows")
    quarter = lax.axis_size("rows") // 4
    starts = (position == quarter) | (position == 3 * quarter)
    ends = (position == quarter - 1) | (position == 3 * quarter - 1)
    is_right = (position < quarter) | (position >= 3 * quarter)
    return starts, ends, is_right


def gather(
    images, cw, lw, vw, feat_a, feat_b, vol_2,
    before, after, there, there_before, there_after, vol_f, conv_2, lift_2, send, recv,
):
    me, size = lax.axis_index("rows"), lax.axis_size("rows")
    up, down, partner = [lax.rem(me + by, size) for by in (1, size - 1, size // 2)]
    starts, ends, _ = place_of()
    rows, cin, cols = images.shape
    halo = rows + 2
    feat = lw.shape[0]
    outc, groups = vw.shape[3:]
    per = feat // groups
    depth = halo * groups
    lane = lax.broadcasted_iota(jnp.int32, (1, cols), 1)

    barrier = pltpu.get_barrier_semaphore()
    for to in (up, down, partner):
        pl.semaphore_signal(barrier, inc=1, device_id={"rows": to}, device_id_type=MESH)
    pl.semaphore_wait(barrier, 3)

    def copy(n, source, target, to):
        return pltpu.make_async_remote_copy(
            src_ref=source,
            dst_ref=target,
            send_sem=send.at[n],
            recv_sem=recv.at[n],
            device_id={"rows": to},
            device_id_type=MESH,
        )

    last, first = pl.ds(rows - 2, 2), pl.ds(0, 2)
    across = copy(0, images, there, partner)
    near = [copy(1, images.at[last], before, up), copy(2, images.at[first], after, down)]
    relays = [copy(3, there.at[last], there_before, up), copy(4, there.at[first], there_after, down)]
    across.start()
    for one in near:
        one.start()

    vol_f[...] = jnp.zeros_like(vol_f)
    for dd in range(3):
        for dc in range(3):
            for r in range(rows):
                for dr in range(3):
                    top = (dc * rows + r) * outc
                    left = dd * depth + (r + dr) * groups
                    vol_f[top : top + outc, left : left + groups] = vw[dr, dd, dc] * (1.0 / per)
    m = 3 * rows * outc
    vol_2[:m], vol_2[m:] = split(vol_f[...])
    wide = jnp.concatenate([cw[dr].reshape(3 * cin, cin) for dr in range(3)], axis=1)
    conv_2[: 3 * cin], conv_2[3 * cin :] = split(wide)
    lift = jnp.concatenate([lw[pl.ds(k, groups, stride=per), :] for k in range(per)], axis=0)
    lift_2[:feat], lift_2[feat:] = split(lift)

    def features(above, middle, below, result, cut):
        parts = []
        for s in range(rows + 4):
            if s < 2:
                x = jnp.where(starts, 0.0, above[s])
            elif s < rows + 2:
                x = middle[s - 2]
            else:
                x = jnp.where(ends, 0.0, below[s - 2 - rows])
            parts.append(split(x))
        for r in range(0, halo, 2):
            pair = (r, min(r + 1, halo - 1))
            hi, lo = [
                jnp.concatenate(
                    [jnp.concatenate([parts[t + k][i] for k in range(3)], axis=0) for t in pair], axis=1
                )
                for i in range(2)
            ]
            y = dot3(conv_2[...], 3 * cin, hi, lo)
            hidden = []
            for n, t in enumerate(pair):
                h = jnp.maximum(taps(y[:, n * cols : (n + 1) * cols], cin, lane), 0.0)
                if cut and t == 0:
                    h = jnp.where(starts, 0.0, h)
                if cut and t == halo - 1:
                    h = jnp.where(ends, 0.0, h)
                hidden.append(h)
            f = dot3(lift_2[...], feat, *split(jnp.concatenate(hidden, axis=1)))
            for n, t in enumerate(pair):
                for k in range(per):
                    part = f[k * groups : (k + 1) * groups, n * cols : (n + 1) * cols]
                    result[k, t * groups : (t + 1) * groups, :] = part

    for one in near:
        one.wait_recv()
    features(before, images, after, feat_a, True)
    across.wait_recv()
    for one in relays:
        one.start()
    for one in relays:
        one.wait_recv()
    features(there_before, there, there_after, feat_b, False)
    for one in (across, *near, *relays):
        one.wait_send()


def compute(first_a, first_b, vol_2, out, feat_a, feat_b, cost_hi, cost_lo):
    _, _, is_right = place_of()
    per, depth, cols = first_a.shape
    m, padded = vol_2.shape
    m = m // 2
    lane = lax.broadcasted_iota(jnp.int32, (1, cols), 1)

    for buf in (cost_hi, cost_lo):
        buf[:depth] = jnp.zeros((depth, cols), bf16)
        tail = buf.shape[0] - (DISP + 1) * depth
        buf[(DISP + 1) * depth :] = jnp.zeros((tail, cols), bf16)
    reach = jnp.where(is_right, cols - 1 - lane, lane)

    def turned(x, by):
        cut = by % cols
        return x if cut == 0 else pltpu.roll(x, jnp.where(is_right, cols - cut, cut), 1)

    def correlate(disparities):
        for base in range(0, depth, 16):
            at = slice(base, base + 16)
            for d in disparities:
                step, b = divmod(d, STEP)
                total = None
                for k in range(per):
                    if b == 0 and step > 0:
                        feat_a[step, k, at, :] = turned(first_a[k, at, :], -STEP * step)
                    if step == 0 and b > 0:
                        feat_b[b, k, at, :] = turned(first_b[k, at, :], b)
                    left = feat_a[step, k, at, :] if step else first_a[k, at, :]
                    term = left * (feat_b[b, k, at, :] if b else first_b[k, at, :])
                    total = term if total is None else total + term
                hi, lo = split(jnp.where(reach >= d, turned(total, STEP * step), 0.0))
                place = (d + 1) * depth + base
                cost_hi[place : place + 16, :] = hi
                cost_lo[place : place + 16, :] = lo

    def filtered(d):
        first, second = d * depth, (d + 1) * depth
        hi, lo = [
            jnp.concatenate([buf[first : first + padded, :], buf[second : second + padded, :]], axis=1)
            for buf in (cost_hi, cost_lo)
        ]
        y = dot3(vol_2[...], m, hi, lo)
        for h in range(2):
            z = taps(y[:, h * cols : (h + 1) * cols], m // 3, lane)
            out[pl.ds(d + h, m // 3, stride=DISP), :] = z

    correlate(range(CHUNK + 2))
    for d in range(0, DISP, CHUNK):
        correlate(range(d + CHUNK + 2, min(d + 2 * CHUNK + 2, DISP)))
        for e in range(d, d + CHUNK, 2):
            filtered(e)


def on_device(images, conv_weight, lift_weight, vol_weight):
    rows, cin, cols = images.shape
    outc, groups = vol_weight.shape[3:]
    feat = lift_weight.shape[0]
    per = feat // groups
    depth = (rows + 2) * groups
    padded = -(-3 * depth // 256) * 256
    m = 3 * rows * outc
    length = DISP * depth + padded
    vmem = pl.BlockSpec(memory_space=pltpu.VMEM)
    edge = pltpu.VMEM((2, cin, cols), f32)
    first_a, first_b, vol_2 = pl.pallas_call(
        gather,
        out_shape=[
            jax.ShapeDtypeStruct((per, depth, cols), f32),
            jax.ShapeDtypeStruct((per, depth, cols), f32),
            jax.ShapeDtypeStruct((2 * m, padded), bf16),
        ],
        in_specs=[vmem] * 4,
        out_specs=[vmem] * 3,
        scratch_shapes=[
            edge,
            edge,
            pltpu.VMEM((rows, cin, cols), f32),
            edge,
            edge,
            pltpu.VMEM((m, padded), f32),
            pltpu.VMEM((6 * cin, 3 * cin), bf16),
            pltpu.VMEM((2 * feat, cin), bf16),
            pltpu.SemaphoreType.DMA((5,)),
            pltpu.SemaphoreType.DMA((5,)),
        ],
        compiler_params=pltpu.CompilerParams(
            vmem_limit_bytes=32 << 20, collective_id=0, has_side_effects=True
        ),
    )(images, conv_weight, lift_weight, vol_weight)
    flat = pl.pallas_call(
        compute,
        out_shape=jax.ShapeDtypeStruct((rows * outc * DISP, cols), f32),
        in_specs=[vmem] * 3,
        out_specs=vmem,
        scratch_shapes=[
            pltpu.VMEM((-(-DISP // STEP), per, depth, cols), f32),
            pltpu.VMEM((STEP, per, depth, cols), f32),
            pltpu.VMEM((length, cols), bf16),
            pltpu.VMEM((length, cols), bf16),
        ],
        compiler_params=pltpu.CompilerParams(vmem_limit_bytes=32 << 20),
    )(first_a, first_b, vol_2)
    return flat.reshape(rows, outc, DISP, cols)


def solution(mesh):
    placed = (P(("scenes", "rows"), None, None), P(), P(), P())
    return jax.shard_map(
        on_device,
        mesh=mesh,
        in_specs=placed,
        out_specs=P(("scenes", "rows"), None, None, None),
        check_vma=False,
    )
```

time: 35.7 us -> 33 us (0.924)
  Pallas kernels: 13.6 us -> 28.8 us
  waiting for transfers between devices: 11.3 us -> 0 us
  starting transfers between devices: 9.63 us -> 0 us
  local copies, waits for them, and re-layouts: 0.01 us -> 3.9 us
  other arithmetic: 0.96 us -> 0 us
    pallas_call x0 -> x1, Pallas kernels: none -> 21.3 us  [on_device(): pl.pallas_call(gather, out_shape=[jax.ShapeDtypeStruct((per, depth, cols)...]
    ppermute x5 -> x0, waiting for transfers between devices: 11.3 us -> none  [shifted(): return lax.ppermute(x, 'rows', [(i, (i + by) % size) for i in range(size)])]
    ppermute x5 -> x0, starting transfers between devices: 9.63 us -> none  [shifted(): return lax.ppermute(x, 'rows', [(i, (i + by) % size) for i in range(size)])]
    pallas_call x1, Pallas kernels: 13.6 us -> 7.53 us  [on_device(): pl.pallas_call(compute, out_shape=jax.ShapeDtypeStruct((rows * outc * DIS...]
    unnamed x6 -> x8, local copies, waits for them, and re-layouts: 0.01 us -> 3.9 us
    concatenate x2 -> x0, other arithmetic: 0.96 us -> none  [framed(): return jnp.concatenate([shifted(x[-2:], 1), x, shifted(x[:2], -1)], axis=0)]
  transfers between devices with their start and end apart: 5 -> 0, of which waited for: 3 -> 0; matrix products, arithmetic and copies ran while one was open for 3% -> 0% of each run, Pallas kernels for 0% -> 0%
where the time goes in v3:
time: 33 us; the launch traced here: 32.7 us
  Pallas kernels  28.8 us (87%)
  local copies, waits for them, and re-layouts  3.9 us (12%)
    pallas_call x1, Pallas kernels, on_device(): pl.pallas_call(gather, out_shape=[jax.ShapeDtypeStruct((per, depth, cols)...  21.3 us
    pallas_call x1, Pallas kernels, on_device(): pl.pallas_call(compute, out_shape=jax.ShapeDtypeStruct((rows * outc * DIS...  7.53 us
    unnamed x8, local copies, waits for them, and re-layouts  3.9 us

profile of v3, /device:TPU:0, one launch (start us, length us, event | category | flops | bytes accessed | tf_op | source)
XLA Modules:
  0.0 32.7 jit_solution(14393341286669854932)
XLA Ops:
  0.0 0.0 copy-start
  0.0 1.1 %copy-done = f32[3,3,128,128]{3,2,1,0:T(8,128)S(1)} copy-done((f32[3,3,128,128]{3,2,1,0:T(8,128)S(1)}, f32[3,3,128,128]{3,2,1,0:T(8,128)}, u32[]{:S(2)}) %copy-start) | copy-done | bytes 589848
  1.1 0.0 copy-start.1
  1.1 1.0 %copy-done.1 = f32[3,3,3,32,40]{4,3,2,1,0:T(8,128)S(1)} copy-done((f32[3,3,3,32,40]{4,3,2,1,0:T(8,128)S(1)}, f32[3,3,3,32,40]{4,3,2,1,0:T(8,128)}, u32[]{:S(2)}) %copy-start.1) | copy-done | bytes 138264
  2.1 0.0 copy-start.2
  2.1 0.9 %copy-done.2 = f32[320,128]{1,0:T(8,128)S(1)} copy-done((f32[320,128]{1,0:T(8,128)S(1)}, f32[320,128]{1,0:T(8,128)}, u32[]{:S(2)}) %copy-start.2) | copy-done | bytes 163864
  3.0 0.0 copy-start.3
  3.0 0.9 %copy-done.3 = f32[2,128,128]{2,1,0:T(8,128)S(1)} copy-done((f32[2,128,128]{2,1,0:T(8,128)S(1)}, f32[2,128,128]{2,1,0:T(8,128)}, u32[]{:S(2)}) %copy-start.3) | copy-done | bytes 131096
  3.9 21.3 %shard_map.46 = (f32[8,160,128]{2,1,0:T(8,128)S(1)}, f32[8,160,128]{2,1,0:T(8,128)S(1)}, bf16[384,512]{1,0:T(8,128)(2,1)S(1)}) custom-call(f32[2,128,128]{2,1,0:T(8,128)S(1)} %copy-done.3, f32[3,3,128,128]{3,2,1,0:T(8,128)S(1)} %copy-done, f32[320,128]{1,0:T(8,128)S(1)} %copy-done.2, f32[3,3,3,32,40]{4,3,2,1,0:T(8,128)S(1)} %copy-done.1), custom_call_target="tpu_custom_call" | custom-call | tf_op jit(solution)/shard_map/pallas_call | solution.py:209
  25.2 7.5 %shard_map.47 = f32[3072,128]{1,0:T(8,128)} custom-call(f32[8,160,128]{2,1,0:T(8,128)S(1)} %get-tuple-element.8.first_a, f32[8,160,128]{2,1,0:T(8,128)S(1)} %get-tuple-element.9.first_b, bf16[384,512]{1,0:T(8,128)(2,1)S(1)} %get-tuple-element.10.vol_2), custom_call_target="tpu_custom_call" | custom-call | tf_op jit(solution)/shard_map/pallas_call | solution.py:234
Async XLA Ops:
  0.0 1.1 %copy-start = (f32[3,3,128,128]{3,2,1,0:T(8,128)S(1)}, f32[3,3,128,128]{3,2,1,0:T(8,128)}, u32[]{:S(2)}) copy-start(f32[3,3,128,128]{3,2,1,0:T(8,128)} %cw.1) | copy-start | bytes 1769476
  1.1 1.0 %copy-start.1 = (f32[3,3,3,32,40]{4,3,2,1,0:T(8,128)S(1)}, f32[3,3,3,32,40]{4,3,2,1,0:T(8,128)}, u32[]{:S(2)}) copy-start(f32[3,3,3,32,40]{4,3,2,1,0:T(8,128)} %vw.1) | copy-start | bytes 414724
  2.1 0.9 %copy-start.2 = (f32[320,128]{1,0:T(8,128)S(1)}, f32[320,128]{1,0:T(8,128)}, u32[]{:S(2)}) copy-start(f32[320,128]{1,0:T(8,128)} %lw.1) | copy-start | bytes 491524
  3.0 0.9 %copy-start.3 = (f32[2,128,128]{2,1,0:T(8,128)S(1)}, f32[2,128,128]{2,1,0:T(8,128)}, u32[]{:S(2)}) copy-start(f32[2,128,128]{2,1,0:T(8,128)} %images.1) | copy-start | bytes 393220

commit v4 on v3

--- a/solution.py
+++ b/solution.py
@@ -31,6 +31,12 @@
     before = jnp.where(lane >= 1, pltpu.roll(y[:size], 1, 1), 0.0)
     after = jnp.where(lane < cols - 1, pltpu.roll(y[2 * size :], cols - 1, 1), 0.0)
     return y[size : 2 * size] + before + after
+
+
+def turned(x, by, is_right):
+    cols = x.shape[-1]
+    cut = by % cols
+    return x if cut == 0 else pltpu.roll(x, jnp.where(is_right, cols - cut, cut), 1)
 
 
 def place_of():
@@ -43,12 +49,14 @@
 
 
 def gather(
-    images, cw, lw, vw, feat_a, feat_b, vol_2,
-    before, after, there, there_before, there_after, vol_f, conv_2, lift_2, send, recv,
+    images, cw_far, lw_far, vw_far, feat_a, feat_b, vol_2,
+    before, after, there, there_before, there_after, vol_f, conv_2, lift_2,
+    here, cw, lw, vw, send, recv, load,
 ):
     me, size = lax.axis_index("rows"), lax.axis_size("rows")
     up, down, partner = [lax.rem(me + by, size) for by in (1, size - 1, size // 2)]
-    starts, ends, _ = place_of()
+    starts, ends, is_right = place_of()
+    half = size // 2
     rows, cin, cols = images.shape
     halo = rows + 2
     feat = lw.shape[0]
@@ -57,16 +65,37 @@
     depth = halo * groups
     lane = lax.broadcasted_iota(jnp.int32, (1, cols), 1)
 
+    to_first, to_last = me == half - 1, me == half
+    from_first, from_last = me == 0, me == size - 1
+    mated = to_first | to_last | from_first | from_last
+    mate = jnp.where(to_first, 0, jnp.where(to_last, size - 1, jnp.where(from_first, half - 1, half)))
+
+    fills = [(vw_far, vw), (cw_far, cw), (lw_far, lw), (images, here)]
+    fills = [pltpu.make_async_copy(x, y, load.at[n]) for n, (x, y) in enumerate(fills)]
+    for one in fills:
+        one.start()
+
     barrier = pltpu.get_barrier_semaphore()
+
+    @pl.when(mated)
+    def _():
+        pl.semaphore_signal(barrier, inc=1, device_id={"rows": mate}, device_id_type=MESH)
+
     for to in (up, down, partner):
         pl.semaphore_signal(barrier, inc=1, device_id={"rows": to}, device_id_type=MESH)
-    pl.semaphore_wait(barrier, 3)
-
-    def copy(n, source, target, to):
+    @pl.when(mated)
+    def _():
+        pl.semaphore_wait(barrier, 4)
+
+    @pl.when(jnp.logical_not(mated))
+    def _():
+        pl.semaphore_wait(barrier, 3)
+
+    def copy(n, source, target, to, out=None):
         return pltpu.make_async_remote_copy(
             src_ref=source,
             dst_ref=target,
-            send_sem=send.at[n],
+            send_sem=send.at[n if out is None else out],
             recv_sem=recv.at[n],
             device_id={"rows": to},
             device_id_type=MESH,
@@ -76,9 +105,25 @@
     across = copy(0, images, there, partner)
     near = [copy(1, images.at[last], before, up), copy(2, images.at[first], after, down)]
     relays = [copy(3, there.at[last], there_before, up), copy(4, there.at[first], there_after, down)]
+    direct = [
+        copy(3, images.at[last], there_before, 0, 5),
+        copy(4, images.at[first], there_after, size - 1, 6),
+    ]
     across.start()
+
+    @pl.when(to_first)
+    def _():
+        direct[0].start()
+
+    @pl.when(to_last)
+    def _():
+        direct[1].start()
+
     for one in near:
         one.start()
+
+    for one in fills:
+        one.wait()
 
     vol_f[...] = jnp.zeros_like(vol_f)
     for dd in range(3):
@@ -128,22 +173,48 @@
                     part = f[k * groups : (k + 1) * groups, n * cols : (n + 1) * cols]
                     result[k, t * groups : (t + 1) * groups, :] = part
 
+    across.wait_recv()
+
+    @pl.when(jnp.logical_not(from_last))
+    def _():
+        relays[0].start()
+
+    @pl.when(jnp.logical_not(from_first))
+    def _():
+        relays[1].start()
+
     for one in near:
         one.wait_recv()
-    features(before, images, after, feat_a, True)
-    across.wait_recv()
-    for one in relays:
-        one.start()
+    features(before, here, after, feat_a.at[0], True)
+    for b in range(1, STEP):
+        for k in range(per):
+            feat_a[b, k] = turned(feat_a[0, k], -b, is_right)
     for one in relays:
         one.wait_recv()
     features(there_before, there, there_after, feat_b, False)
-    for one in (across, *near, *relays):
+    for one in (across, *near):
         one.wait_send()
 
-
-def compute(first_a, first_b, vol_2, out, feat_a, feat_b, cost_hi, cost_lo):
+    @pl.when(jnp.logical_not(from_last))
+    def _():
+        relays[0].wait_send()
+
+    @pl.when(jnp.logical_not(from_first))
+    def _():
+        relays[1].wait_send()
+
+    @pl.when(to_first)
+    def _():
+        direct[0].wait_send()
+
+    @pl.when(to_last)
+    def _():
+        direct[1].wait_send()
+
+
+def compute(feat_a, first_b, vol_2, out, feat_b, cost_hi, cost_lo):
     _, _, is_right = place_of()
-    per, depth, cols = first_a.shape
+    per, depth, cols = first_b.shape
     m, padded = vol_2.shape
     m = m // 2
     lane = lax.broadcasted_iota(jnp.int32, (1, cols), 1)
@@ -153,10 +224,6 @@
         tail = buf.shape[0] - (DISP + 1) * depth
         buf[(DISP + 1) * depth :] = jnp.zeros((tail, cols), bf16)
     reach = jnp.where(is_right, cols - 1 - lane, lane)
-
-    def turned(x, by):
-        cut = by % cols
-        return x if cut == 0 else pltpu.roll(x, jnp.where(is_right, cols - cut, cut), 1)
 
     def correlate(disparities):
         for base in range(0, depth, 16):
@@ -166,13 +233,11 @@
                 total = None
                 for k in range(per):
                     if b == 0 and step > 0:
-                        feat_a[step, k, at, :] = turned(first_a[k, at, :], -STEP * step)
-                    if step == 0 and b > 0:
-                        feat_b[b, k, at, :] = turned(first_b[k, at, :], b)
-                    left = feat_a[step, k, at, :] if step else first_a[k, at, :]
-                    term = left * (feat_b[b, k, at, :] if b else first_b[k, at, :])
+                        feat_b[step, k, at, :] = turned(first_b[k, at, :], STEP * step, is_right)
+                    right = feat_b[step, k, at, :] if step else first_b[k, at, :]
+                    term = feat_a[b, k, at, :] * right
                     total = term if total is None else total + term
-                hi, lo = split(jnp.where(reach >= d, turned(total, STEP * step), 0.0))
+                hi, lo = split(jnp.where(reach >= d, turned(total, b, is_right), 0.0))
                 place = (d + 1) * depth + base
                 cost_hi[place : place + 16, :] = hi
                 cost_lo[place : place + 16, :] = lo
@@ -209,11 +274,11 @@
     first_a, first_b, vol_2 = pl.pallas_call(
         gather,
         out_shape=[
-            jax.ShapeDtypeStruct((per, depth, cols), f32),
+            jax.ShapeDtypeStruct((STEP, per, depth, cols), f32),
             jax.ShapeDtypeStruct((per, depth, cols), f32),
             jax.ShapeDtypeStruct((2 * m, padded), bf16),
         ],
-        in_specs=[vmem] * 4,
+        in_specs=[pl.BlockSpec(memory_space=pltpu.HBM)] * 4,
         out_specs=[vmem] * 3,
         scratch_shapes=[
             edge,
@@ -224,8 +289,13 @@
             pltpu.VMEM((m, padded), f32),
             pltpu.VMEM((6 * cin, 3 * cin), bf16),
             pltpu.VMEM((2 * feat, cin), bf16),
+            pltpu.VMEM(images.shape, f32),
+            pltpu.VMEM(conv_weight.shape, f32),
+            pltpu.VMEM(lift_weight.shape, f32),
+            pltpu.VMEM(vol_weight.shape, f32),
+            pltpu.SemaphoreType.DMA((7,)),
             pltpu.SemaphoreType.DMA((5,)),
-            pltpu.SemaphoreType.DMA((5,)),
+            pltpu.SemaphoreType.DMA((4,)),
         ],
         compiler_params=pltpu.CompilerParams(
             vmem_limit_bytes=32 << 20, collective_id=0, has_side_effects=True
@@ -238,7 +308,6 @@
         out_specs=vmem,
         scratch_shapes=[
             pltpu.VMEM((-(-DISP // STEP), per, depth, cols), f32),
-            pltpu.VMEM((STEP, per, depth, cols), f32),
             pltpu.VMEM((length, cols), bf16),
             pltpu.VMEM((length, cols), bf16),
         ],

time: 33 us -> 30.4 us (0.921)
  the two profiles are of different devices: /device:TPU:0 before, /device:TPU:1 now
where the time goes in v4:
time: 30.4 us; the launch traced here: 30.2 us
  Pallas kernels  26.3 us (87%)
  local copies, waits for them, and re-layouts  3.9 us (13%)
    pallas_call x1, Pallas kernels, on_device(): pl.pallas_call(gather, out_shape=[jax.ShapeDtypeStruct((STEP, per, depth,...  19.3 us
    pallas_call x1, Pallas kernels, on_device(): pl.pallas_call(compute, out_shape=jax.ShapeDtypeStruct((rows * outc * DIS...  6.93 us
    unnamed x8, local copies, waits for them, and re-layouts  3.9 us

profile of v4, /device:TPU:1, one launch (start us, length us, event | category | flops | bytes accessed | tf_op | source)
XLA Modules:
  0.0 30.2 jit_solution(15748937878911069756)
XLA Ops:
  0.0 0.0 copy-start
  0.0 1.1 %copy-done = f32[3,3,128,128]{3,2,1,0:T(8,128)S(1)} copy-done((f32[3,3,128,128]{3,2,1,0:T(8,128)S(1)}, f32[3,3,128,128]{3,2,1,0:T(8,128)}, u32[]{:S(2)}) %copy-start) | copy-done | bytes 589848
  1.1 0.0 copy-start.1
  1.1 1.0 %copy-done.1 = f32[3,3,3,32,40]{4,3,2,1,0:T(8,128)S(1)} copy-done((f32[3,3,3,32,40]{4,3,2,1,0:T(8,128)S(1)}, f32[3,3,3,32,40]{4,3,2,1,0:T(8,128)}, u32[]{:S(2)}) %copy-start.1) | copy-done | bytes 138264
  2.1 0.0 copy-start.2
  2.1 0.9 %copy-done.2 = f32[320,128]{1,0:T(8,128)S(1)} copy-done((f32[320,128]{1,0:T(8,128)S(1)}, f32[320,128]{1,0:T(8,128)}, u32[]{:S(2)}) %copy-start.2) | copy-done | bytes 163864
  3.0 0.0 copy-start.3
  3.0 0.9 %copy-done.3 = f32[2,128,128]{2,1,0:T(8,128)S(1)} copy-done((f32[2,128,128]{2,1,0:T(8,128)S(1)}, f32[2,128,128]{2,1,0:T(8,128)}, u32[]{:S(2)}) %copy-start.3) | copy-done | bytes 131096
  3.9 19.3 %shard_map.46 = (f32[8,8,160,128]{3,2,1,0:T(8,128)S(1)}, f32[8,160,128]{2,1,0:T(8,128)S(1)}, bf16[384,512]{1,0:T(8,128)(2,1)S(1)}) custom-call(f32[2,128,128]{2,1,0:T(8,128)S(1)} %copy-done.3, f32[3,3,128,128]{3,2,1,0:T(8,128)S(1)} %copy-done, f32[320,128]{1,0:T(8,128)S(1)} %copy-done.2, f32[3,3,3,32,40]{4,3,2,1,0:T(8,128)S(1)} %copy-done.1), custom_call_target="tpu_custom_call" | custom-call | tf_op jit(solution)/shard_map/pallas_call | solution.py:274
  23.2 6.9 %shard_map.47 = f32[3072,128]{1,0:T(8,128)} custom-call(f32[8,8,160,128]{3,2,1,0:T(8,128)S(1)} %get-tuple-element.8.feat_a, f32[8,160,128]{2,1,0:T(8,128)S(1)} %get-tuple-element.9.first_b, bf16[384,512]{1,0:T(8,128)(2,1)S(1)} %get-tuple-element.10.vol_2), custom_call_target="tpu_custom_call" | custom-call | tf_op jit(solution)/shard_map/pallas_call | solution.py:304
Async XLA Ops:
  0.0 1.1 %copy-start = (f32[3,3,128,128]{3,2,1,0:T(8,128)S(1)}, f32[3,3,128,128]{3,2,1,0:T(8,128)}, u32[]{:S(2)}) copy-start(f32[3,3,128,128]{3,2,1,0:T(8,128)} %cw_far.1) | copy-start | bytes 1769476
  1.1 1.0 %copy-start.1 = (f32[3,3,3,32,40]{4,3,2,1,0:T(8,128)S(1)}, f32[3,3,3,32,40]{4,3,2,1,0:T(8,128)}, u32[]{:S(2)}) copy-start(f32[3,3,3,32,40]{4,3,2,1,0:T(8,128)} %vw_far.1) | copy-start | bytes 414724
  2.1 0.9 %copy-start.2 = (f32[320,128]{1,0:T(8,128)S(1)}, f32[320,128]{1,0:T(8,128)}, u32[]{:S(2)}) copy-start(f32[320,128]{1,0:T(8,128)} %lw_far.1) | copy-start | bytes 491524
  3.0 0.9 %copy-start.3 = (f32[2,128,128]{2,1,0:T(8,128)S(1)}, f32[2,128,128]{2,1,0:T(8,128)}, u32[]{:S(2)}) copy-start(f32[2,128,128]{2,1,0:T(8,128)} %images.1) | copy-start | bytes 393220
